TPU v7x, 32 devices: a whole 2x2x4 slice. The times are simulated.
32 devices in a mesh: dp: 8 (over y, x, core), tensor: 4 (over z).
Axes of the slice: x: 2, y: 2, z: 4, core: 2. Of those that a mesh axis runs over, the one named last changes fastest.
Arguments:
- inputs: bfloat16 [16384, 768], P('dp'), may hold values from -6 to 6
- w_qkv: bfloat16 [768, 3, 768], P(None, None, 'tensor'), may hold values from -0.3125 to 0.3125
- b_qv: float32 [2, 768], P(None, 'tensor'), may hold values from -3 to 3
- w_out: bfloat16 [768, 768], P('tensor'), may hold values from -1.25 to 1.25
- b_out: float32 [768], replicated, may hold values from -3 to 3
- g_one: float32 [768], replicated, may hold values from 0.5 to 1.5
- s_one: float32 [768], replicated, may hold values from -3 to 3
- w_up: bfloat16 [768, 3072], P(None, 'tensor'), may hold values from -0.21875 to 0.21875
- b_up: float32 [3072], P('tensor'), may hold values from -3 to 3
- w_down: bfloat16 [3072, 768], P('tensor'), may hold values from -0.15625 to 0.15625
- b_down: float32 [768], replicated, may hold values from -3 to 3
- g_two: float32 [768], replicated, may hold values from 0.5 to 1.5
- s_two: float32 [768], replicated, may hold values from -3 to 3
- cotangent: bfloat16 [16384, 768], P('dp'), may hold values from -6 to 6
- pad_mask: int32 [16384], P('dp'), may hold values 0 or 1
- doc_lengths: int32 [32], P('dp'), may hold values from 30 to 512, as said below
Outputs:
- out: bfloat16 [16384, 768], P('dp')
- d_inputs: float32 [16384, 768], P('dp')
- d_w_qkv: float32 [768, 3, 768], P(None, None, 'tensor')
- d_b_qv: float32 [2, 768], P(None, 'tensor')
- d_w_out: float32 [768, 768], P('tensor')
- d_b_out: float32 [768], replicated
- d_g_one: float32 [768], replicated
- d_s_one: float32 [768], replicated
- d_w_up: float32 [768, 3072], P(None, 'tensor')
- d_b_up: float32 [3072], P('tensor')
- d_w_down: float32 [3072, 768], P('tensor')
- d_b_down: float32 [768], replicated
- d_g_two: float32 [768], replicated
- d_s_two: float32 [768], replicated
Inputs may be any that keep to these rules, and one draw needn't show every extreme that they name: `doc_lengths`: in every draw one document has 512 true tokens and one has 30. Rows at or beyond a document's count are padding: they are no keys whatever pad_mask says, and their outputs are zero. The first token of a document is always a key.
All inputs are finite; a program needn't handle non-finite values. No bound on the sum of `pad_mask` on one device may be relied on, other than what follows from the above.
Results may differ from a plain program's by a relative error of at most 0.014.
The roundings to bfloat16 on the way count: a program that leaves them out, or rounds other values in their place, can miss the bound.
Values may be sent and summed in bfloat16 or wider, within the bound.
No kernel may reach another device: no remote copies, remote signals or barrier semaphores. Data moves between devices by JAX's collectives and lax.ppermute only.
A program may use at most 128 MiB of HBM per device.

v0:
```python
import jax
import jax.numpy as jnp
from jax import lax
from jax.sharding import PartitionSpec as P

HD = 64


def norm_layer(values, gain, shift):
    center = values - jnp.mean(values, axis=-1, keepdims=True)
    spread = jnp.mean(center * center, axis=-1, keepdims=True)
    return center * lax.rsqrt(spread + 1e-05) * gain + shift


def gelu_exact(values):
    return jax.nn.gelu(values, approximate=False)


def masked_scores(queries, key_rows, key_valid):
    scores = jnp.einsum("qhe,khe->hqk", queries, key_rows, preferred_element_type=jnp.float32)
    return jnp.where(key_valid[None, None, :], scores, -1e30)


def doc_forward(packed):
    queries, key_rows, values, key_valid = packed
    scores = masked_scores(queries, key_rows, key_valid)
    log_total = jax.nn.logsumexp(scores, axis=-1, keepdims=True)
    weights = jnp.exp(scores - log_total).astype(jnp.bfloat16)
    context = jnp.einsum("hqk,khe->qhe", weights, values, preferred_element_type=jnp.float32)
    return (context.astype(jnp.bfloat16), log_total)


def doc_backward(packed):
    queries, key_rows, values, key_valid, log_total, d_context = packed
    scores = masked_scores(queries, key_rows, key_valid)
    weights = jnp.exp(scores - log_total)
    d_prob = jnp.einsum("qhe,khe->hqk", d_context, values, preferred_element_type=jnp.float32)
    d_values = jnp.einsum(
        "hqk,qhe->khe", weights.astype(jnp.bfloat16), d_context, preferred_element_type=jnp.float32
    )
    d_scores = (weights * (d_prob - jnp.sum(d_prob * weights, axis=-1, keepdims=True))).astype(
        jnp.bfloat16
    )
    d_query = jnp.einsum("hqk,khe->qhe", d_scores, key_rows, preferred_element_type=jnp.float32)
    d_keys = jnp.einsum("hqk,qhe->khe", d_scores, queries, preferred_element_type=jnp.float32)
    return (
        d_query.astype(jnp.bfloat16),
        d_keys.astype(jnp.bfloat16),
        d_values.astype(jnp.bfloat16),
    )


def per_device(
    inputs,
    w_qkv,
    b_qv,
    w_out,
    b_out,
    g_one,
    s_one,
    w_up,
    b_up,
    w_down,
    b_down,
    g_two,
    s_two,
    cotangent,
    pad_mask,
    doc_lengths,
):
    rows = inputs.shape[0]
    doc_count = doc_lengths.shape[0]
    length = rows // doc_count
    local_heads = w_qkv.shape[2] // HD
    scale = HD ** (-0.5)
    position = jnp.arange(length, dtype=jnp.int32)
    inside = position[None, :] < doc_lengths[:, None]
    key_valid = inside & ((pad_mask.reshape(doc_count, length) == 1) | (position[None, :] == 0))
    row_weight = inside.astype(jnp.float32).reshape(rows, 1)
    projected = jnp.einsum("td,dce->tce", inputs, w_qkv, preferred_element_type=jnp.float32)
    queries = ((projected[:, 0] + b_qv[0]) * scale).astype(jnp.bfloat16)
    key_rows = projected[:, 1].astype(jnp.bfloat16)
    values = (projected[:, 2] + b_qv[1]).astype(jnp.bfloat16)
    shaped = (doc_count, length, local_heads, HD)
    queries_doc = queries.reshape(shaped)
    keys_doc = key_rows.reshape(shaped)
    values_doc = values.reshape(shaped)
    context, log_total = lax.map(doc_forward, (queries_doc, keys_doc, values_doc, key_valid))
    context = context.reshape(rows, local_heads * HD)
    heads_part = jnp.dot(context, w_out, preferred_element_type=jnp.float32)
    attn = lax.psum(heads_part, "tensor")
    z_one = inputs.astype(jnp.float32) + attn + b_out
    h_one, pull_one = jax.vjp(norm_layer, z_one, g_one, s_one)
    h_low = h_one.astype(jnp.bfloat16)
    up_value = jnp.dot(h_low, w_up, preferred_element_type=jnp.float32) + b_up
    act, pull_act = jax.vjp(gelu_exact, up_value)
    act_low = act.astype(jnp.bfloat16)
    down_part = jnp.dot(act_low, w_down, preferred_element_type=jnp.float32)
    down = lax.psum(down_part, "tensor")
    z_two = h_one + down + b_down
    normed, pull_two = jax.vjp(norm_layer, z_two, g_two, s_two)
    d_ztwo, d_gtwo, d_stwo = pull_two(cotangent.astype(jnp.float32) * row_weight)
    d_bdown = jnp.sum(d_ztwo, axis=0)
    result = (normed * row_weight).astype(jnp.bfloat16)
    dz_two_low = d_ztwo.astype(jnp.bfloat16)
    d_wdown = jnp.einsum("tf,td->fd", act_low, dz_two_low, preferred_element_type=jnp.float32)
    d_act = jnp.einsum("td,fd->tf", dz_two_low, w_down, preferred_element_type=jnp.float32)
    d_up_low = pull_act(d_act)[0].astype(jnp.bfloat16)
    d_bup = jnp.sum(d_up_low, axis=0, dtype=jnp.float32)
    d_wup = jnp.einsum("td,tf->df", h_low, d_up_low, preferred_element_type=jnp.float32)
    hone_part = jnp.einsum("tf,df->td", d_up_low, w_up, preferred_element_type=jnp.float32)
    d_hone = lax.psum(hone_part, "tensor") + d_ztwo
    d_zone, d_gone, d_sone = pull_one(d_hone)
    d_bout = jnp.sum(d_zone, axis=0)
    dz_one_low = d_zone.astype(jnp.bfloat16)
    d_wout = jnp.einsum("th,td->hd", context, dz_one_low, preferred_element_type=jnp.float32)
    d_context = jnp.einsum(
        "td,hd->th", dz_one_low, w_out, preferred_element_type=jnp.float32
    ).astype(jnp.bfloat16)
    back_items = (
        queries_doc,
        keys_doc,
        values_doc,
        key_valid,
        log_total,
        d_context.reshape(shaped),
    )
    d_query, d_keys, d_values = lax.map(doc_backward, back_items)
    d_query = d_query.reshape(rows, local_heads * HD) * jnp.asarray(scale, jnp.bfloat16)
    stacked = jnp.stack(
        [d_query, d_keys.reshape(rows, local_heads * HD), d_values.reshape(rows, local_heads * HD)],
        axis=1,
    )
    d_wqkv = jnp.einsum("td,tce->dce", inputs, stacked, preferred_element_type=jnp.float32)
    d_bqv = jnp.stack(
        [
            jnp.sum(stacked[:, 0], axis=0, dtype=jnp.float32),
            jnp.sum(stacked[:, 2], axis=0, dtype=jnp.float32),
        ]
    )
    input_part = jnp.einsum("tce,dce->td", stacked, w_qkv, preferred_element_type=jnp.float32)
    d_inputs = lax.psum(input_part, "tensor") + d_zone
    summed = lax.psum(
        (
            d_wqkv,
            d_bqv,
            d_wout,
            d_bout,
            d_gone,
            d_sone,
            d_wup,
            d_bup,
            d_wdown,
            d_bdown,
            d_gtwo,
            d_stwo,
        ),
        "dp",
    )
    return (
        result,
        d_inputs,
        summed[0],
        summed[1],
        summed[2],
        summed[3],
        summed[4],
        summed[5],
        summed[6],
        summed[7],
        summed[8],
        summed[9],
        summed[10],
        summed[11],
    )


def solution(mesh):
    placed = (
        P("dp", None),
        P(None, None, "tensor"),
        P(None, "tensor"),
        P("tensor", None),
        P(),
        P(),
        P(),
        P(None, "tensor"),
        P("tensor"),
        P("tensor", None),
        P(),
        P(),
        P(),
        P("dp", None),
        P("dp"),
        P("dp"),
    )
    return jax.shard_map(
        per_device,
        mesh=mesh,
        in_specs=placed,
        out_specs=(
            P("dp", None),
            P("dp", None),
            P(None, None, "tensor"),
            P(None, "tensor"),
            P("tensor", None),
            P(),
            P(),
            P(),
            P(None, "tensor"),
            P("tensor"),
            P("tensor", None),
            P(),
            P(),
            P(),
        ),
        check_vma=False,
    )
```

profile of v0, /device:TPU:0, one launch (start us, length us, event | category | flops | bytes accessed | tf_op | source)
XLA Modules:
  0.0 1201.6 jit_solution(13847251560515117021)
XLA Ops:
  7.2 4.2 fusion.90
  13.5 3.1 squeeze.34
  16.6 2.2 squeeze.35
  21.1 2.9 fusion.73
  25.0 13.6 %while.26 = (s32[]{:T(128)}, bf16[4,512,3,64]{1,3,2,0:T(8,128)(2,1)}, f32[4,3,512,1]{2,1,3,0:T(4,128)}, bf16[4,512,3,64]{1,3,2,0:T(8,128)(2,1)S(1)}, pred[4,512]...) while((s32[]{:T(128)}, ...), condition=%wide.region_3.4_spmd, body=%wide.region_0.3_spmd.sunk | while | flops 207728640 | bytes 10306649 | solution.py:88
  30.3 1.5 fusion.134
  38.6 2.0 copy.49
  41.7 4.7 fusion.91
  46.9 225.2 %all-reduce.8.cloned.1.call-done = f32[2048,768]{1,0:T(8,128)} async-done(((f32[2048,768]{1,0:T(8,128)}), f32[2048,768]{1,0:T(8,128)}) %all-reduce.8.cloned.1.call-update) | async-done | bytes 6291472 | tf_op jit(solution)/shard_map/psum | solution.py:91
  272.2 4.6 fusion.88
  279.4 18.3 %multiply_convert_fusion.2 = (bf16[2048,768]{1,0:T(8,128)(2,1)S(1)}, f32[2048,768]{1,0:T(8,128)}, f32[2048,768]{1,0:T(8,128)}) fusion(f32[768]{0:T(1024)S(1)} %copy-done.35, bf16[2048,768]{1,0:T(8,128)(2,1)S(1)} %fusion.69, bf16[768,768]{1,0:T(8,128)(2,1)S(1)} %copy-done), kind=kOutput, calls=%fused_computation.84 | convolution fusion | flops 2519728128 | bytes 20057088 | tf_op jit(solution)/shard_map/dot_general | solution.py:95
  297.8 1.8 copy-done.37
  299.5 4.5 fusion.92
  304.2 221.7 %all-reduce.10.cloned.1.call-done = f32[2048,768]{1,0:T(8,128)} async-done(((f32[2048,768]{1,0:T(8,128)}), f32[2048,768]{1,0:T(8,128)}) %all-reduce.10.cloned.1.call-update) | async-done | bytes 6291472 | tf_op jit(solution)/shard_map/psum | solution.py:99
  525.9 5.7 fusion.86
  533.5 3.6 multiply_reduce_fusion.1
  537.2 4.9 fusion.85
  542.1 9.3 convert_reduce_fusion
  551.4 1.7 copy-done.36
  553.1 4.5 fusion.93
  557.9 221.6 %all-reduce.12.cloned.1.call-done = f32[2048,768]{1,0:T(8,128)} async-done(((f32[2048,768]{1,0:T(8,128)}), f32[2048,768]{1,0:T(8,128)}) %all-reduce.12.cloned.1.call-update) | async-done | bytes 6291472 | tf_op jit(solution)/shard_map/psum | solution.py:112
  779.5 8.7 multiply_reduce_fusion.2
  788.3 4.3 fusion.84
  792.6 2.7 copy-done.3
  799.3 30.5 %while.27 = (s32[]{:T(128)}, bf16[4,512,3,64]{1,3,2,0:T(8,128)(2,1)S(1)}, bf16[4,512,3,64]{1,3,2,0:T(8,128)(2,1)}, bf16[4,512,3,64]{1,3,2,0:T(8,128)(2,1)S(1)}, ...) while((s32[]{:T(128)}, ...), condition=%wide.region_17.18_spmd, body=%wide.region_15.17_spmd.sunk | while | flops 513047040 | bytes 25611892 | solution.py:128
  800.7 2.0 multiply_reduce_fusion.8
  805.2 1.7 fusion.147
  808.3 2.0 multiply_reduce_fusion.8
  812.8 1.7 fusion.147
  816.0 2.0 multiply_reduce_fusion.8
  820.5 1.7 fusion.147
  823.6 2.0 multiply_reduce_fusion.8
  828.1 1.7 fusion.147
  830.6 1.5 mul.219
  832.0 2.1 constant_dynamic-update-slice_fusion.2
  835.3 1.5 copy.54
  836.8 2.3 stack_reshape.7
  841.1 7.2 convolution_bitcast_fusion
  848.3 7.1 fusion.94
  855.4 7.1 fusion.81
  862.6 1.8 fusion.83
  865.4 3.2 fusion.75
  870.1 200.1 %all-reduce.14.cloned.1.call-done = f32[2048,768]{1,0:T(8,128)} async-done(((f32[2048,768]{1,0:T(8,128)}), f32[2048,768]{1,0:T(8,128)}) %all-reduce.14.cloned.1.call-update) | async-done | bytes 6291472 | tf_op jit(solution)/shard_map/psum | solution.py:142
  1070.1 7.7 add_reduce_fusion
  1077.8 26.2 %all-reduce = (f32[2,192]{1,0:T(2,128)}, f32[768]{0:T(1024)}, f32[768]{0:T(1024)}, f32[768]{0:T(1024)}, f32[768]{0:T(1024)}, /*index=5*/f32[768]{0:T(1024)}, f32[768]{0:T(1024)}, f32[768]{0:T(1024)}) all-reduce(f32[2,192]{1,0:T(2,128)S(1)} %pad_maximum_fusion, ...), channel_id=1, replica_groups=mesh['dp'=8,'tensor'=4] {'dp'}, use_global_device_ids=true, to_apply=%region_22.23 | all-reduce | flops 5760 | bytes 46080 | tf_op jit(solution)/shard_map/psum | solution.py:143
  1104.1 82.9 %all-reduce.16.cloned.1.call-done = (f32[768,3,192]{0,2,1:T(8,128)}, f32[192,768]{1,0:T(8,128)}, f32[768,768]{1,0:T(8,128)}, f32[768,768]{1,0:T(8,128)}) async-done(((f32[768,3,192]{0,2,1:T(8,128)}, f32[192,768]{1,0:T(8,128)}, f32[768,768]{1,0:T(8,128)}, f32[768,768]{1,0:T(8,128)}), (f32[768,3,192]{0,2,1:T(8,128)}, f32[192,768]{1,0:T(8,128)}, f32[768,768]{1,0:T(8,128)}, ...) | async-done | bytes 7077904 | tf_op jit(solution)/shard_map/psum | solution.py:143
  1187.0 2.9 copy.107
  1189.9 1.9 copy.108
  (191 shorter events, 52.3 us)
Async XLA Ops:
  7.2 272.2 %copy-start = (bf16[768,768]{1,0:T(8,128)(2,1)S(1)}, bf16[768,768]{1,0:T(8,128)(2,1)}, u32[]{:S(2)}) copy-start(bf16[768,768]{1,0:T(8,128)(2,1)} %param.27) | copy-start | bytes 3538948
  7.2 265.0 %all-reduce.8.cloned.1.call-start = ((), (), s32[]{:S(2)}) async-start(), calls=%async_computation | async-start | bytes 12582912 | tf_op jit(solution)/shard_map/psum | solution.py:91
  11.5 7.3 copy-start.32
  12.8 7.5 copy-start.27
  38.6 7.8 copy-start.10
  40.8 0.9 copy-start.6
  41.7 230.5 %copy-start.29 = (f32[768]{0:T(1024)S(1)}, f32[768]{0:T(1024)}, u32[]{:S(2)}) copy-start(f32[768]{0:T(1024)} %param.24) | copy-start | bytes 9220
  46.4 479.5 %all-reduce.10.cloned.1.call-start = ((), (), s32[]{:S(2)}) async-start(), calls=%async_computation.1 | async-start | bytes 12582912 | tf_op jit(solution)/shard_map/psum | solution.py:99
  276.8 2.7 copy-start.2
  276.8 0.9 copy-start.18
  276.8 0.9 copy-start.23
  277.7 1.8 copy-start.35
  279.4 18.3 %copy-start.12 = (bf16[2048,768]{1,0:T(8,128)(2,1)}, bf16[2048,768]{1,0:T(8,128)(2,1)S(1)}, u32[]{:S(2)}) copy-start(bf16[2048,768]{1,0:T(8,128)(2,1)S(1)} %fusion.69) | copy-start | bytes 9437188
  279.4 20.1 %copy-start.33 = (bf16[768,768]{1,0:T(8,128)(2,1)S(1)}, bf16[768,768]{1,0:T(8,128)(2,1)}, u32[]{:S(2)}) copy-start(bf16[768,768]{1,0:T(8,128)(2,1)} %param.29) | copy-start | bytes 3538948
  297.8 1.8 copy-start.37
  304.0 221.9 %copy-start.30 = (f32[768]{0:T(1024)S(1)}, f32[768]{0:T(1024)}, u32[]{:S(2)}) copy-start(f32[768]{0:T(1024)} %param.30) | copy-start | bytes 9220
  304.0 475.5 %all-reduce.12.cloned.1.call-start = ((), (), s32[]{:S(2)}) async-start(), calls=%async_computation.2 | async-start | bytes 12582912 | tf_op jit(solution)/shard_map/psum | solution.py:112
  531.6 1.9 copy-start.5
  531.6 1.9 copy-start.22
  532.5 4.6 copy-start.31
  533.5 8.5 slice-start.2
  537.1 4.9 copy-start.34
  537.1 4.9 slice-start.3
  542.0 9.4 copy-start.4
  542.0 237.5 %copy-start.19 = (f32[2048]{0:T(1024)}, f32[2048]{0:T(1024)S(1)}, u32[]{:S(2)}) copy-start(f32[2048]{0:T(1024)S(1)} %negate_multiply_fusion.2) | copy-start | bytes 24580
  551.4 1.7 copy-start.36
  557.6 512.5 %all-reduce.14.cloned.1.call-start = ((), (), s32[]{:S(2)}) async-start(), calls=%async_computation.3 | async-start | bytes 12582912 | tf_op jit(solution)/shard_map/psum | solution.py:142
  788.3 7.0 copy-start.16
  792.6 2.7 copy-start.3
  829.8 9.3 copy-start.8
  829.9 4.3 copy-start.11
  848.2 7.1 copy-start.20
  848.3 338.7 %all-reduce.16.cloned.1.call-start = ((), (), s32[]{:S(2)}) async-start(), calls=%async_computation.4 | async-start | bytes 14155776 | tf_op jit(solution)/shard_map/psum | solution.py:143
  848.3 7.1 copy-start.38
  848.3 14.2 %slice-start = ((s8[6291456]{0:T(1024)(128)(4,1)}), s8[4194304]{0:T(1024)(128)(4,1)S(1)}, s32[]{:S(2)}) async-start(s8[6291456]{0:T(1024)(128)(4,1)} %bitcast.157), calls=%async_computation.5 | async-start | bytes 8388608
  855.4 7.1 slice-start.1
  855.4 7.1 copy-start.7
  862.5 1.9 copy-start.13
  862.5 2.8 copy-start.17
  868.6 1.1 copy-start.9
  870.0 207.8 %copy-start.21 = (f32[768]{0:T(1024)S(1)}, f32[768]{0:T(1024)}, u32[]{:S(2)}) copy-start(f32[768]{0:T(1024)} %get-tuple-element.150) | copy-start | bytes 9220
  870.0 207.8 %copy-start.24 = (f32[768]{0:T(1024)S(1)}, f32[768]{0:T(1024)}, u32[]{:S(2)}) copy-start(f32[768]{0:T(1024)} %get-tuple-element.145) | copy-start | bytes 9220
  870.1 207.8 %copy-start.25 = (f32[768]{0:T(1024)S(1)}, f32[768]{0:T(1024)}, u32[]{:S(2)}) copy-start(f32[768]{0:T(1024)} %get-tuple-element.149) | copy-start | bytes 9220
  870.1 207.7 %copy-start.26 = (f32[768]{0:T(1024)S(1)}, f32[768]{0:T(1024)}, u32[]{:S(2)}) copy-start(f32[768]{0:T(1024)} %get-tuple-element.215) | copy-start | bytes 9220
  870.1 207.7 %copy-start.28 = (f32[768]{0:T(1024)S(1)}, f32[768]{0:T(1024)}, u32[]{:S(2)}) copy-start(f32[768]{0:T(1024)} %get-tuple-element.223) | copy-start | bytes 9220
  1187.0 4.9 copy-start.15
  1187.0 6.3 copy-start.14
  1187.0 7.7 copy-start.1
Sparse Core Ops, SparseCore 0:
  46.5 225.5 all-reduce.7
  304.1 221.7 all-reduce.9
  557.8 221.7 all-reduce.11
  848.4 221.7 all-reduce.13
  1074.8 112.0 all-reduce.15
where the time goes:
time: 1210 us; the launch traced here: 1200 us
  waiting for transfers between devices  952 us (79%)
  matrix products  106 us (9%)
  other arithmetic  55.1 us (5%)
  local copies, waits for them, and re-layouts  46.6 us (4%)
  blocking collectives  26.2 us (2%)
  between operations  14.8 us (1%)
    psum x1, waiting for transfers between devices, per_device(): attn = lax.psum(heads_part, 'tensor')  225 us
    psum x1, waiting for transfers between devices, per_device(): down = lax.psum(down_part, 'tensor')  222 us
    psum x1, waiting for transfers between devices, per_device(): d_hone = lax.psum(hone_part, 'tensor') + d_ztwo  222 us
    psum x1, waiting for transfers between devices, per_device(): d_inputs = lax.psum(input_part, 'tensor') + d_zone  200 us
    psum x1, waiting for transfers between devices, per_device(): lax.psum((d_wqkv, d_bqv, d_wout, d_bout, d_gone, d_sone, d_wup, d_bup, d_...  82.9 us
    psum x1, blocking collectives, per_device(): lax.psum((d_wqkv, d_bqv, d_wout, d_bout, d_gone, d_sone, d_wup, d_bup, d_...  26.2 us
  transfers between devices with their start and end apart: 5, of which 5 were waited for; matrix products, arithmetic and copies ran while one was open for 2% of the time, Pallas kernels for 0%

commit v1 on v0

--- a/solution.py
+++ b/solution.py
@@ -109,7 +109,7 @@
     d_bup = jnp.sum(d_up_low, axis=0, dtype=jnp.float32)
     d_wup = jnp.einsum("td,tf->df", h_low, d_up_low, preferred_element_type=jnp.float32)
     hone_part = jnp.einsum("tf,df->td", d_up_low, w_up, preferred_element_type=jnp.float32)
-    d_hone = lax.psum(hone_part, "tensor") + d_ztwo
+    d_hone = jnp.sum(lax.all_gather(hone_part, "tensor"), axis=0) + d_ztwo
     d_zone, d_gone, d_sone = pull_one(d_hone)
     d_bout = jnp.sum(d_zone, axis=0)
     dz_one_low = d_zone.astype(jnp.bfloat16)

time: 1210 us -> 1430 us (1.18)
  waiting for transfers between devices: 952 us -> 1150 us
    all_gather x0 -> x1, waiting for transfers between devices: none -> 424 us  [per_device(): d_hone = jnp.sum(lax.all_gather(hone_part, 'tensor'), axis=0) + d_ztwo]
    psum x1 -> x0, waiting for transfers between devices: 222 us -> none  [per_device(): d_hone = lax.psum(hone_part, 'tensor') + d_ztwo]
where the time goes in v1:
time: 1430 us; the launch traced here: 1420 us
  waiting for transfers between devices  1150 us (80%)
  matrix products  105 us (7%)
  other arithmetic  67.3 us (5%)
  local copies, waits for them, and re-layouts  51.5 us (4%)
  blocking collectives  26.2 us (2%)
  between operations  14.5 us (1%)
    all_gather x1, waiting for transfers between devices, per_device(): d_hone = jnp.sum(lax.all_gather(hone_part, 'tensor'), axis=0) + d_ztwo  424 us
    psum x1, waiting for transfers between devices, per_device(): attn = lax.psum(heads_part, 'tensor')  225 us
    psum x1, waiting for transfers between devices, per_device(): down = lax.psum(down_part, 'tensor')  221 us
    psum x1, waiting for transfers between devices, per_device(): d_inputs = lax.psum(input_part, 'tensor') + d_zone  199 us
    psum x1, waiting for transfers between devices, per_device(): lax.psum((d_wqkv, d_bqv, d_wout, d_bout, d_gone, d_sone, d_wup, d_bup, d_...  82.9 us
  transfers between devices with their start and end apart: 5, of which 5 were waited for; matrix products, arithmetic and copies ran while one was open for 2% of the time, Pallas kernels for 0%

profile of v1, /device:TPU:0, one launch (start us, length us, event | category | flops | bytes accessed | tf_op | source)
XLA Modules:
  0.0 1418.6 jit_solution(17263611825293018730)
XLA Ops:
  7.8 4.1 fusion.90
  14.7 3.1 squeeze.35
  20.6 2.2 squeeze.34
  23.6 2.9 fusion.73
  27.5 13.6 while.26
  41.1 2.0 copy.49
  44.2 4.7 fusion.91
  49.3 225.4 %all-reduce.7.cloned.1.call-done = f32[2048,768]{1,0:T(8,128)} async-done(((f32[2048,768]{1,0:T(8,128)}), f32[2048,768]{1,0:T(8,128)}) %all-reduce.7.cloned.1.call-update) | async-done | bytes 6291472 | tf_op jit(solution)/shard_map/psum | solution.py:91
  274.7 4.6 fusion.88
  282.0 18.3 %multiply_convert_fusion.2 = (bf16[2048,768]{1,0:T(8,128)(2,1)S(1)}, f32[2048,768]{1,0:T(8,128)}, f32[2048,768]{1,0:T(8,128)}) fusion(f32[768]{0:T(1024)S(1)} %copy-done.30, bf16[2048,768]{1,0:T(8,128)(2,1)S(1)} %fusion.69, bf16[768,768]{1,0:T(8,128)(2,1)S(1)} %copy-done), kind=kOutput, calls=%fused_computation.84 | convolution fusion | flops 2519728128 | bytes 20057088 | tf_op jit(solution)/shard_map/dot_general | solution.py:95
  300.3 1.7 copy-done.32
  302.0 4.5 fusion.92
  307.1 221.3 %all-reduce.9.cloned.1.call-done = f32[2048,768]{1,0:T(8,128)} async-done(((f32[2048,768]{1,0:T(8,128)}), f32[2048,768]{1,0:T(8,128)}) %all-reduce.9.cloned.1.call-update) | async-done | bytes 6291472 | tf_op jit(solution)/shard_map/psum | solution.py:99
  528.4 5.7 fusion.86
  536.0 3.6 multiply_reduce_fusion.1
  539.7 4.9 fusion.85
  544.6 9.3 convert_reduce_fusion
  553.9 1.7 copy-done.31
  555.6 4.5 fusion.93
  560.2 424.2 %all-gather.3.cloned.1.call-done = f32[8192,768]{1,0:T(8,128)} async-done(((f32[2048,768]{1,0:T(8,128)}), f32[8192,768]{1,0:T(8,128)}) %all-gather.3.cloned.1.call-update) | async-done | bytes 25165840 | tf_op jit(solution)/shard_map/all_gather | solution.py:112
  984.4 12.9 reduce_sum.186
  997.2 8.1 multiply_reduce_fusion.2
  1005.4 4.3 fusion.84
  1009.7 2.7 copy-done.3
  1016.4 30.5 %while.27 = (s32[]{:T(128)}, bf16[4,512,3,64]{1,3,2,0:T(8,128)(2,1)S(1)}, bf16[4,512,3,64]{1,3,2,0:T(8,128)(2,1)}, bf16[4,512,3,64]{1,3,2,0:T(8,128)(2,1)S(1)}, ...) while((s32[]{:T(128)}, ...), condition=%wide.region_17.18_spmd, body=%wide.region_15.17_spmd.sunk | while | flops 513047040 | bytes 25611900 | solution.py:128
  1017.8 1.7 fusion.147
  1019.5 2.0 multiply_reduce_fusion.8
  1025.4 1.7 fusion.147
  1027.2 2.0 multiply_reduce_fusion.8
  1033.0 1.8 fusion.147
  1034.8 2.0 multiply_reduce_fusion.8
  1040.7 1.7 fusion.147
  1042.4 2.0 multiply_reduce_fusion.8
  1046.9 2.0 copy.53
  1049.6 1.5 copy.54
  1051.1 2.1 stack_reshape.7
  1054.7 3.0 mul.219
  1060.4 5.7 convolution_bitcast_fusion
  1066.3 7.1 fusion.94
  1073.3 7.1 fusion.81
  1080.5 1.8 fusion.83
  1083.3 3.2 fusion.75
  1088.1 199.3 %all-reduce.11.cloned.1.call-done = f32[2048,768]{1,0:T(8,128)} async-done(((f32[2048,768]{1,0:T(8,128)}), f32[2048,768]{1,0:T(8,128)}) %all-reduce.11.cloned.1.call-update) | async-done | bytes 6291472 | tf_op jit(solution)/shard_map/psum | solution.py:142
  1287.4 7.7 add_reduce_fusion
  1295.0 26.2 %all-reduce = (f32[2,192]{1,0:T(2,128)}, f32[768]{0:T(1024)}, f32[768]{0:T(1024)}, f32[768]{0:T(1024)}, f32[768]{0:T(1024)}, /*index=5*/f32[768]{0:T(1024)}, f32[768]{0:T(1024)}, f32[768]{0:T(1024)}) all-reduce(f32[2,192]{1,0:T(2,128)S(1)} %pad_maximum_fusion, ...), channel_id=1, replica_groups=mesh['dp'=8,'tensor'=4] {'dp'}, use_global_device_ids=true, to_apply=%region_22.23 | all-reduce | flops 5760 | bytes 46080 | tf_op jit(solution)/shard_map/psum | solution.py:143
  1321.2 82.9 %all-reduce.13.cloned.1.call-done = (f32[768,3,192]{0,2,1:T(8,128)}, f32[192,768]{1,0:T(8,128)}, f32[768,768]{1,0:T(8,128)}, f32[768,768]{1,0:T(8,128)}) async-done(((f32[768,3,192]{0,2,1:T(8,128)}, f32[192,768]{1,0:T(8,128)}, f32[768,768]{1,0:T(8,128)}, f32[768,768]{1,0:T(8,128)}), (f32[768,3,192]{0,2,1:T(8,128)}, f32[192,768]{1,0:T(8,128)}, f32[768,768]{1,0:T(8,128)}, ...) | async-done | bytes 7077904 | tf_op jit(solution)/shard_map/psum | solution.py:143
  1404.2 2.9 copy.106
  1407.1 1.9 copy.107
  (182 shorter events, 57.4 us)
Async XLA Ops:
  7.2 274.8 %copy-start = (bf16[768,768]{1,0:T(8,128)(2,1)S(1)}, bf16[768,768]{1,0:T(8,128)(2,1)}, u32[]{:S(2)}) copy-start(bf16[768,768]{1,0:T(8,128)(2,1)} %param.27) | copy-start | bytes 3538948
  7.2 267.5 %all-reduce.7.cloned.1.call-start = ((), (), s32[]{:S(2)}) async-start(), calls=%async_computation | async-start | bytes 12582912 | tf_op jit(solution)/shard_map/psum | solution.py:91
  11.9 1.5 copy-start.22
  11.9 2.1 copy-start.27
  41.1 7.8 copy-start.10
  43.3 0.9 copy-start.6
  44.2 230.5 %copy-start.24 = (f32[768]{0:T(1024)S(1)}, f32[768]{0:T(1024)}, u32[]{:S(2)}) copy-start(f32[768]{0:T(1024)} %param.24) | copy-start | bytes 9220
  48.9 479.5 %all-reduce.9.cloned.1.call-start = ((), (), s32[]{:S(2)}) async-start(), calls=%async_computation.1 | async-start | bytes 12582912 | tf_op jit(solution)/shard_map/psum | solution.py:99
  279.3 2.7 copy-start.2
  279.3 0.9 copy-start.18
  279.3 0.9 copy-start.21
  280.2 1.8 copy-start.30
  282.0 18.3 %copy-start.11 = (bf16[2048,768]{1,0:T(8,128)(2,1)}, bf16[2048,768]{1,0:T(8,128)(2,1)S(1)}, u32[]{:S(2)}) copy-start(bf16[2048,768]{1,0:T(8,128)(2,1)S(1)} %fusion.69) | copy-start | bytes 9437188
  282.0 20.0 %copy-start.28 = (bf16[768,768]{1,0:T(8,128)(2,1)S(1)}, bf16[768,768]{1,0:T(8,128)(2,1)}, u32[]{:S(2)}) copy-start(bf16[768,768]{1,0:T(8,128)(2,1)} %param.29) | copy-start | bytes 3538948
  300.3 1.7 copy-start.32
  306.5 221.9 %copy-start.25 = (f32[768]{0:T(1024)S(1)}, f32[768]{0:T(1024)}, u32[]{:S(2)}) copy-start(f32[768]{0:T(1024)} %param.30) | copy-start | bytes 9220
  306.5 677.9 %all-gather.3.cloned.1.call-start = ((), (), s32[]{:S(2)}) async-start(), calls=%async_computation.3 | async-start | bytes 31457280 | tf_op jit(solution)/shard_map/all_gather | solution.py:112
  534.1 1.9 copy-start.5
  534.1 1.9 copy-start.20
  535.0 4.6 copy-start.26
  536.0 8.5 slice-start.2
  539.6 4.9 copy-start.29
  539.6 4.9 slice-start.3
  544.5 9.4 copy-start.4
  553.9 1.7 copy-start.31
  560.2 727.2 %all-reduce.11.cloned.1.call-start = ((), (), s32[]{:S(2)}) async-start(), calls=%async_computation.2 | async-start | bytes 12582912 | tf_op jit(solution)/shard_map/psum | solution.py:142
  1005.4 7.0 copy-start.15
  1009.7 2.7 copy-start.3
  1046.9 12.0 copy-start.8
  1059.0 1.4 copy-start.16
  1066.2 338.0 %all-reduce.13.cloned.1.call-start = ((), (), s32[]{:S(2)}) async-start(), calls=%async_computation.4 | async-start | bytes 14155776 | tf_op jit(solution)/shard_map/psum | solution.py:143
  1066.3 7.1 copy-start.33
  1066.3 14.2 %slice-start = ((s8[6291456]{0:T(1024)(128)(4,1)}), s8[4194304]{0:T(1024)(128)(4,1)S(1)}, s32[]{:S(2)}) async-start(s8[6291456]{0:T(1024)(128)(4,1)} %bitcast.158), calls=%async_computation.5 | async-start | bytes 8388608
  1073.3 7.2 slice-start.1
  1073.3 7.2 copy-start.7
  1080.5 1.9 copy-start.12
  1080.5 2.8 copy-start.17
  1086.6 1.1 copy-start.9
  1088.0 207.0 %copy-start.19 = (f32[768]{0:T(1024)S(1)}, f32[768]{0:T(1024)}, u32[]{:S(2)}) copy-start(f32[768]{0:T(1024)} %get-tuple-element.150) | copy-start | bytes 9220
  1088.1 207.0 %copy-start.23 = (f32[768]{0:T(1024)S(1)}, f32[768]{0:T(1024)}, u32[]{:S(2)}) copy-start(f32[768]{0:T(1024)} %get-tuple-element.223) | copy-start | bytes 9220
  1404.2 4.9 copy-start.14
  1404.2 6.3 copy-start.13
  1404.2 7.7 copy-start.1
Sparse Core Ops, SparseCore 0:
  49.1 225.5 all-reduce.6
  306.6 221.7 all-reduce.8
  560.3 424.0 all-gather.2
  1066.3 221.0 all-reduce.10
  1292.1 112.0 all-reduce.12
